TPU v7x, 32 devices: a whole 2x2x4 slice. The times are simulated.
32 devices in a mesh: dp: 16 (over z, y, core), tensor: 2 (over x).
Axes of the slice: x: 2, y: 2, z: 4, core: 2. Of those that a mesh axis runs over, the one named last changes fastest.
Arguments:
- tokens: bfloat16 [6144, 2880], P('dp', 'tensor'), may hold values from -6 to 6
- out_grad: bfloat16 [6144, 2880], P('dp', 'tensor'), may hold values from -6 to 6
- route_probs: bfloat16 [6144, 4], P('dp'), may hold values from 0.099609375 to 1
- expert_ids: int32 [6144, 4], P('dp'), may hold values from 0 to 63, all different within a row; in each aligned block of 384 rows (0 to 383, 384 to 767, ...) at most 36 rows name the same one
- placement_map: int32 [64], replicated, may hold values from 0 to 63, each once
- w_gate: bfloat16 [16, 2880, 2880], P('dp', None, 'tensor'), may hold values from -0.109375 to 0.109375
- w_up: bfloat16 [16, 2880, 2880], P('dp', None, 'tensor'), may hold values from -0.109375 to 0.109375
- w_down: bfloat16 [16, 2880, 2880], P('dp', 'tensor'), may hold values from -0.109375 to 0.109375
Outputs:
- input_grad: bfloat16 [6144, 2880], P('dp', 'tensor')
- gate_grad: bfloat16 [16, 2880, 2880], P('dp', None, 'tensor')
- up_grad: bfloat16 [16, 2880, 2880], P('dp', None, 'tensor')
- down_grad: bfloat16 [16, 2880, 2880], P('dp', 'tensor')
- prob_grad: bfloat16 [6144, 4], P('dp')
Inputs may be any that keep to these rules, and one draw needn't show every extreme that they name: `expert_ids`: each row names 4 different experts. In the rows of one index of dp no expert is named by more than 36 rows, a bound that some block reaches. `placement_map`: A permutation: every value is taken by exactly one expert.
All inputs are finite; a program needn't handle non-finite values.
Results may differ from a plain program's by a relative error of at most 0.011.
Values may be sent and summed in bfloat16 or wider, within the bound.
A program may use at most 128 MiB of HBM per device.

v0:
```python
import jax
import jax.numpy as jnp
from jax import lax
from jax.sharding import PartitionSpec as P

EXP_OWN = 4
SWISH_SLOPE = 1.702


def route_layout(expert_ids, placement_map, owners, capacity):
    tok_rows, top_count = expert_ids.shape
    experts = placement_map.shape[0]
    per_owner = experts // owners
    matches = expert_ids[:, :, None] == jnp.arange(experts, dtype=jnp.int32)[None, None, :]
    code_value = jnp.sum(jnp.where(matches, placement_map[None, None, :], 0), axis=-1).reshape(-1)
    in_wave = code_value % per_owner == 0
    owner_of = code_value // per_owner
    chosen = (
        (owner_of[:, None] == jnp.arange(owners, dtype=jnp.int32)[None, :]) & in_wave[:, None]
    ).astype(jnp.int32)
    before = jnp.cumsum(chosen, axis=0) - chosen
    slot_index = jnp.sum(before * chosen, axis=1)
    target = jnp.where(in_wave, owner_of * capacity + slot_index, owners * capacity)
    slot_route = (
        jnp.full((owners * capacity,), -1, jnp.int32)
        .at[target]
        .set(jnp.arange(tok_rows * top_count, dtype=jnp.int32), mode="drop")
    )
    return (in_wave, target, slot_route)


def build_rows(values, slot_route, row_valid, top_count):
    picked = jnp.take(values, jnp.where(row_valid, slot_route // top_count, 0), axis=0)
    return jnp.where(row_valid[:, None], picked, jnp.zeros_like(picked))


def shards(tokens, out_grad, route_probs, expert_ids, placement_map, w_gate, w_up, w_down):
    owners = lax.axis_size("dp")
    tok_rows, top_count = expert_ids.shape
    capacity = 3 * tok_rows * top_count // (2 * EXP_OWN * owners)
    in_wave, target, slot_route = route_layout(expert_ids, placement_map, owners, capacity)
    row_valid = slot_route >= 0
    safe_route = jnp.where(row_valid, slot_route, 0)
    zero_half = jnp.zeros((), jnp.bfloat16)
    prob_rows = jnp.where(row_valid, route_probs.reshape(-1)[safe_route], zero_half)
    part_width = tokens.shape[1]
    send_x = build_rows(tokens, slot_route, row_valid, top_count).reshape(
        owners, capacity, part_width
    )
    send_d = build_rows(out_grad, slot_route, row_valid, top_count).reshape(
        owners, capacity, part_width
    )
    got_x, got_d, got_p = (
        lax.all_to_all(send_x, "dp", split_axis=0, concat_axis=0, tiled=True),
        lax.all_to_all(send_d, "dp", split_axis=0, concat_axis=0, tiled=True),
        lax.all_to_all(
            prob_rows.reshape(owners, capacity), "dp", split_axis=0, concat_axis=0, tiled=True
        ),
    )
    rows_x, rows_d = (
        lax.all_gather(got_x.reshape(owners * capacity, part_width), "tensor", axis=1, tiled=True),
        lax.all_gather(got_d.reshape(owners * capacity, part_width), "tensor", axis=1, tiled=True),
    )
    prob_column = got_p.reshape(-1).astype(jnp.float32)[:, None]
    gate_w = w_gate[0]
    up_w = w_up[0]
    down_w = w_down[0]
    contract_cols = (((1,), (1,)), ((), ()))
    contract_rows = (((0,), (0,)), ((), ()))
    gate_pre = jnp.dot(rows_x, gate_w, preferred_element_type=jnp.float32)
    up_pre = jnp.dot(rows_x, up_w, preferred_element_type=jnp.float32)
    sig_gate = jax.nn.sigmoid(SWISH_SLOPE * gate_pre)
    active = (gate_pre * sig_gate * (up_pre + 1.0)).astype(jnp.bfloat16)
    down_back = lax.dot_general(rows_d, down_w, contract_cols, preferred_element_type=jnp.float32)
    outputs = jnp.dot(active, down_w, preferred_element_type=jnp.float32)
    slice_sum = jnp.sum(rows_d.astype(jnp.float32) * outputs, axis=1)
    prob_sum = lax.psum(slice_sum, "tensor")
    delta_act = prob_column * down_back
    grad_gate_pre = (
        delta_act
        * (up_pre + 1.0)
        * (sig_gate + SWISH_SLOPE * gate_pre * sig_gate * (1.0 - sig_gate))
    ).astype(jnp.bfloat16)
    grad_up_pre = (delta_act * gate_pre * sig_gate).astype(jnp.bfloat16)
    scaled_grad = (prob_column * rows_d.astype(jnp.float32)).astype(jnp.bfloat16)
    down_grad = lax.dot_general(
        active, scaled_grad, contract_rows, preferred_element_type=jnp.float32
    ).astype(jnp.bfloat16)
    gate_grad = lax.dot_general(
        rows_x, grad_gate_pre, contract_rows, preferred_element_type=jnp.float32
    ).astype(jnp.bfloat16)
    up_grad = lax.dot_general(
        rows_x, grad_up_pre, contract_rows, preferred_element_type=jnp.float32
    ).astype(jnp.bfloat16)
    input_part = lax.dot_general(
        grad_gate_pre, gate_w, contract_cols, preferred_element_type=jnp.float32
    ) + lax.dot_general(grad_up_pre, up_w, contract_cols, preferred_element_type=jnp.float32)
    rounded_part = lax.optimization_barrier(input_part.astype(jnp.bfloat16)).astype(jnp.float32)
    input_rows = lax.psum_scatter(
        rounded_part.astype(jnp.bfloat16), "tensor", scatter_dimension=1, tiled=True
    )
    part_cols = input_rows.shape[1]
    back_rows, back_prob = (
        lax.all_to_all(
            input_rows.reshape(owners, capacity, part_cols),
            "dp",
            split_axis=0,
            concat_axis=0,
            tiled=True,
        ),
        lax.all_to_all(
            prob_sum.astype(jnp.bfloat16).reshape(owners, capacity),
            "dp",
            split_axis=0,
            concat_axis=0,
            tiled=True,
        ),
    )
    back_rows = back_rows.reshape(owners * capacity, part_cols)
    back_prob = back_prob.reshape(-1)
    safe_target = jnp.where(in_wave, target, 0)
    route_rows = jnp.where(in_wave[:, None], jnp.take(back_rows, safe_target, axis=0), zero_half)
    input_grad = jnp.sum(
        route_rows.reshape(tok_rows, top_count, part_cols).astype(jnp.float32), axis=1
    ).astype(jnp.bfloat16)
    prob_grad = jnp.where(in_wave, back_prob[safe_target], zero_half).reshape(tok_rows, top_count)
    return (input_grad, gate_grad[None], up_grad[None], down_grad[None], prob_grad)


def solution(mesh):
    in_specs = (
        P("dp", "tensor"),
        P("dp", "tensor"),
        P("dp", None),
        P("dp", None),
        P(),
        P("dp", None, "tensor"),
        P("dp", None, "tensor"),
        P("dp", "tensor", None),
    )
    out_specs = (
        P("dp", "tensor"),
        P("dp", None, "tensor"),
        P("dp", None, "tensor"),
        P("dp", "tensor", None),
        P("dp", None),
    )
    return jax.shard_map(shards, mesh=mesh, in_specs=in_specs, out_specs=out_specs, check_vma=False)
```

profile of v0, /device:TPU:13, one launch (start us, length us, event | category | flops | bytes accessed | tf_op | source)
XLA Modules:
  0.0 413.7 jit_solution(8770292031321615427)
XLA Ops:
  7.2 0.9 select_reduce_fusion.1
  8.2 0.1 copy.36
  8.3 0.2 reshape.287
  8.4 0.1 reshape.285
  8.6 0.1 reshape.284
  8.8 4.5 %reduce-window.6 = s32[16,12,128]{2,1,0:T(8,128)S(1)} reduce-window(s32[16,12,128]{2,1,0:T(8,128)S(1)} %fusion.30, s32[]{:T(128)} %constant.77.clone.1), window={size=1x1x128 pad=0_0x0_0x127_0}, to_apply=%region_1.2 | reduce-window | flops 3121152 | bytes 196612 | tf_op jit(solution)/shard_map/reduce-window
  13.4 0.4 slice_reduce_fusion
  13.8 0.2 reduce-window.9
  14.0 0.1 broadcast_add_fusion
  14.2 0.7 fusion.40
  14.8 6.2 %scatter_custom_fusion = s32[576]{0:T(1024)S(1)} fusion(s32[1536]{0:T(1024)S(1)} %get-tuple-element.22, s32[1536]{0:T(1024)S(1)} %iota.15, s32[]{:T(128)} %constant.82.clone.1), kind=kCustom, calls=%fused_computation.111 | custom fusion | bytes 2308 | tf_op jit(solution)/shard_map/scatter | solution.py:27
  21.1 1.6 copy.45
  22.7 1.2 copy.43
  23.9 3.6 gather_fusion.4
  27.5 3.6 gather_fusion.3
  31.1 3.8 select_select_fusion
  34.8 2.6 reshape.291
  37.5 50.9 %all_to_all.35 = bf16[16,36,1440]{2,1,0:T(8,128)(2,1)} all-to-all(bf16[16,36,1440]{2,1,0:T(8,128)(2,1)S(1)} %reshape.291), channel_id=1, replica_groups=mesh['dp'=16,'tensor'=2] {'dp'}, dimensions={0} | all-to-all | bytes 3317760 | tf_op jit(solution)/shard_map/all_to_all | solution.py:54
  88.4 3.8 reshape.292
  92.2 2.6 reshape.289
  94.9 49.4 %all_to_all.36 = bf16[16,36,1440]{2,1,0:T(8,128)(2,1)} all-to-all(bf16[16,36,1440]{2,1,0:T(8,128)(2,1)S(1)} %reshape.289), channel_id=1, replica_groups=mesh['dp'=16,'tensor'=2] {'dp'}, dimensions={0} | all-to-all | bytes 3317760 | tf_op jit(solution)/shard_map/all_to_all | solution.py:55
  144.2 3.8 reshape.290
  148.1 0.2 copy.41
  148.3 0.2 reshape.288
  148.5 3.9 gather_fusion
  152.5 0.1 all_to_all.28
  152.6 9.0 %all_to_all.37 = bf16[16,1,36]{2,1,0:T(2,128)(2,1)S(1)} all-to-all(bf16[16,1,36]{2,1,0:T(2,128)(2,1)S(1)} %all_to_all.28), channel_id=1, replica_groups=mesh['dp'=16,'tensor'=2] {'dp'}, dimensions={0} | all-to-all | bytes 2304 | tf_op jit(solution)/shard_map/all_to_all | solution.py:56
  161.6 0.7 reshape.296
  162.2 5.6 %copy.46 = bf16[2,1440,576]{1,0,2:T(2,128)(2,1)S(1)} copy(bf16[2,1440,576]{1,2,0:T(8,128)(2,1)} %all-gather.7.cloned.1.call-done) | data formatting | bytes 6635520 | tf_op jit(solution)/shard_map/all_gather | solution.py:61
  167.9 4.1 %reshape.351 = bf16[2880,576]{0,1:T(8,128)(2,1)} reshape(bf16[2,1440,576]{1,0,2:T(2,128)(2,1)S(1)} %copy.46) | data formatting | bytes 6635520
  172.0 25.0 %all-gather.5.cloned.1.call-done = bf16[2,1440,576]{1,2,0:T(8,128)(2,1)} async-done(((bf16[1,1440,576]{1,2,0:T(8,128)(2,1)}), bf16[2,1440,576]{1,2,0:T(8,128)(2,1)}) %all-gather.5.cloned.1.call-update) | async-done | bytes 3317776 | tf_op jit(solution)/shard_map/all_gather | solution.py:62
  197.0 5.6 %copy.44 = bf16[2,1440,576]{1,0,2:T(2,128)(2,1)S(1)} copy(bf16[2,1440,576]{1,2,0:T(8,128)(2,1)} %all-gather.5.cloned.1.call-done) | data formatting | bytes 6635520 | tf_op jit(solution)/shard_map/all_gather | solution.py:62
  202.7 4.2 %reshape.349 = bf16[2880,576]{0,1:T(8,128)(2,1)} reshape(bf16[2,1440,576]{1,0,2:T(2,128)(2,1)S(1)} %copy.44) | data formatting | bytes 6635520
  206.8 11.2 %fusion.5 = f32[576,1440]{1,0:T(8,128)} fusion(bf16[2880,576]{0,1:T(8,128)(2,1)} %reshape.351, bf16[1,2880,1440]{1,2,0:T(8,128)(2,1)} %param.15), kind=kOutput, calls=%fused_computation.14 | convolution fusion | flops 4777574400 | bytes 14929920 | tf_op jit(solution)/shard_map/dot_general | solution.py:70
  218.0 19.8 %fusion.21 = f32[576,1440]{1,0:T(8,128)S(1)} fusion(bf16[2880,576]{0,1:T(8,128)(2,1)S(1)} %copy-done.4, bf16[1,1440,2880]{2,1,0:T(8,128)(2,1)} %param.17, f32[576]{0:T(1024)S(1)} %copy-done.8), kind=kOutput, calls=%fused_computation.30 | convolution fusion | flops 4778403840 | bytes 14932224 | tf_op jit(solution)/shard_map/dot_general | solution.py:74
  237.8 12.5 %multiply_convert_fusion = (bf16[576,1440]{1,0:T(8,128)(2,1)}, bf16[576,1440]{1,0:T(8,128)(2,1)}, bf16[576,1440]{1,0:T(8,128)(2,1)S(1)}) fusion(f32[576,1440]{1,0:T(8,128)} %fusion.5, f32[576,1440]{1,0:T(8,128)S(1)} %fusion.21, bf16[2880,576]{0,1:T(8,128)(2,1)S(1)} %copy-done.1, bf16[1,2880,1440]{1,2,0:T(8,128)(2,1)} %param.16), kind=kOutput, calls=%fused_computation.31 | convolution fusion | flops 4792504320 | bytes 23224320 | tf_op jit(solution)/shard_map/dot_general | solution.py:71
  250.3 9.3 %fusion.3 = f32[576,2880]{1,0:T(8,128)S(1)} fusion(bf16[576,1440]{1,0:T(8,128)(2,1)} %get-tuple-element.30, bf16[1,2880,1440]{1,2,0:T(8,128)(2,1)} %param.15), kind=kOutput, calls=%fused_computation.12 | convolution fusion | flops 4777574400 | bytes 16588800 | tf_op jit(solution)/shard_map/dot_general | solution.py:95
  259.7 9.5 %add_convert_fusion = bf16[576,2880]{1,0:T(8,128)(2,1)S(1)} fusion(f32[576,2880]{1,0:T(8,128)S(1)} %fusion.3, bf16[576,1440]{1,0:T(8,128)(2,1)S(1)} %get-tuple-element.31, bf16[1,2880,1440]{1,2,0:T(8,128)(2,1)} %param.16), kind=kOutput, calls=%fused_computation.28 | convolution fusion | flops 4780892160 | bytes 19906560 | tf_op jit(solution)/shard_map/dot_general | solution.py:97
  269.2 3.7 copy.50
  273.0 0.2 reduce_sum.45
  273.2 0.4 copy-done.7
  273.6 9.5 %fusion.16 = f32[576]{0:T(1024)S(1)} fusion(bf16[2880,576]{0,1:T(8,128)(2,1)} %reshape.349, bf16[576,1440]{1,0:T(8,128)(2,1)} %get-tuple-element.29, bf16[1,1440,2880]{2,1,0:T(8,128)(2,1)} %param.17), kind=kOutput, calls=%fused_computation.27 | convolution fusion | flops 4782550528 | bytes 13273344 | tf_op jit(solution)/shard_map/dot_general | solution.py:75
  283.1 4.4 %psum.7 = bf16[576]{0:T(1024)(128)(2,1)S(1)} all-reduce(f32[576]{0:T(1024)S(1)} %fusion.16), channel_id=1, replica_groups=mesh['dp'=16,'tensor'=2] {'tensor'}, use_global_device_ids=true, to_apply=%region_8.10 | all-reduce | flops 576 | bytes 3456 | tf_op jit(solution)/shard_map/psum | solution.py:77
  287.5 0.7 all_to_all.29
  288.2 7.3 %all-to-all-start.4 = ((bf16[16,1,36]{2,1,0:T(2,128)(2,1)}), bf16[16,1,36]{2,1,0:T(2,128)(2,1)S(1)}, u32[]{:S(2)}, u32[]{:S(2)}) async-start(bf16[16,1,36]{2,1,0:T(2,128)(2,1)} %all_to_all.29), calls=%async_computation.4 | async-start | bytes 16384 | tf_op jit(solution)/shard_map/all_to_all | solution.py:111
  295.5 10.8 %fusion.2 = bf16[1,2880,1440]{1,2,0:T(8,128)(2,1)} fusion(bf16[2880,576]{0,1:T(8,128)(2,1)S(1)} %copy-done.2, bf16[576,1440]{1,0:T(8,128)(2,1)} %copy-done.10), kind=kOutput, calls=%fused_computation.11 | convolution fusion | flops 4781721600 | bytes 13271040 | tf_op jit(solution)/shard_map/dot_general | solution.py:92
  306.3 16.3 %reduce-scatter.4.cloned.1.call-done = bf16[1440,576]{1,0:T(8,128)(2,1)} async-done(((bf16[2880,576]{1,0:T(8,128)(2,1)}), bf16[1440,576]{1,0:T(8,128)(2,1)}) %reduce-scatter.4.cloned.1.call-update) | async-done | bytes 1658896
  322.6 2.6 copy.51
  325.2 1.6 reshape.293
  326.8 7.1 %all-to-all-start.3 = ((bf16[16,36,1440]{2,1,0:T(8,128)(2,1)}), bf16[16,36,1440]{2,1,0:T(8,128)(2,1)}, u32[]{:S(2)}, u32[]{:S(2)}) async-start(bf16[16,36,1440]{2,1,0:T(8,128)(2,1)} %reshape.293), calls=%async_computation.3 | async-start | bytes 3932160 | tf_op jit(solution)/shard_map/all_to_all | solution.py:104
  333.9 10.9 %fusion.1 = bf16[1,2880,1440]{1,2,0:T(8,128)(2,1)} fusion(bf16[2880,576]{0,1:T(8,128)(2,1)S(1)} %copy-done.3, bf16[576,1440]{1,0:T(8,128)(2,1)} %get-tuple-element.30), kind=kOutput, calls=%fused_computation.10 | convolution fusion | flops 4781721600 | bytes 13271040 | tf_op jit(solution)/shard_map/dot_general | solution.py:89
  344.9 9.5 %fusion = bf16[1,1440,2880]{2,1,0:T(8,128)(2,1)} fusion(bf16[576,1440]{1,0:T(8,128)(2,1)S(1)} %copy-done.11, bf16[2880,576]{0,1:T(8,128)(2,1)S(1)} %copy-done.5, f32[576]{0:T(1024)S(1)} %copy-done.8), kind=kOutput, calls=%fused_computation.9 | convolution fusion | flops 4786698240 | bytes 13273344 | tf_op jit(solution)/shard_map/dot_general | solution.py:86
  354.4 0.1 reshape.295
  354.5 9.5 %gather_fusion.2 = bf16[1536]{0:T(1024)(128)(2,1)S(1)} fusion(bf16[576]{0:T(1024)(128)(2,1)S(1)} %reshape.295, s32[2048]{0:T(1024)S(1)} %pad_clamp_fusion), kind=kCustom, calls=%fused_computation.4 | custom fusion | bytes 12288 | tf_op jit(solution)/shard_map/gather | solution.py:126
  364.0 0.2 gather.21
  364.3 0.6 broadcast_select_fusion
  364.9 0.2 copy.35
  365.1 0.2 copy.39
  365.3 13.1 %all-to-all-done.3 = bf16[16,36,1440]{2,1,0:T(8,128)(2,1)} async-done(((bf16[16,36,1440]{2,1,0:T(8,128)(2,1)}), bf16[16,36,1440]{2,1,0:T(8,128)(2,1)}, u32[]{:S(2)}, u32[]{:S(2)}) %all-to-all-start.3) | async-done | bytes 1658912 | tf_op jit(solution)/shard_map/all_to_all | solution.py:104
  378.5 2.7 reshape.294
  381.2 6.2 %gather_fusion.1 = bf16[1536,1440]{1,0:T(8,128)(2,1)} fusion(bf16[576,1440]{1,0:T(8,128)(2,1)S(1)} %reshape.294, s32[2048]{0:T(1024)S(1)} %pad_clamp_fusion), kind=kCustom, calls=%fused_computation.3 | custom fusion | bytes 8853504 | tf_op jit(solution)/shard_map/jit(_take)/gather | solution.py:122
  387.4 8.9 %gather.19 = bf16[384,4,1440]{2,1,0:T(4,128)(2,1)} reshape(bf16[1536,1440]{1,0:T(8,128)(2,1)} %gather_fusion.1) | data formatting | bytes 8847360 | tf_op jit(solution)/shard_map/jit(_take)/gather | solution.py:122
  396.3 9.1 %select_reduce_fusion = bf16[384,1440]{1,0:T(8,128)(2,1)S(1)} fusion(bf16[384,4,1440]{2,1,0:T(4,128)(2,1)} %gather.19, pred[384,4]{1,0:T(8,128)(4,1)S(1)} %copy.39, pred[384,4]{1,0:T(8,128)(4,1)S(1)} %copy.35), kind=kLoop, calls=%fused_computation.29 | loop fusion | flops 6082560 | bytes 5532672 | tf_op jit(solution)/shard_map/reduce_sum | solution.py:123
  405.4 1.4 copy.49
  (49 shorter events, 0.6 us)
Async XLA Ops:
  7.2 15.5 %copy-start.6 = (bf16[384,1440]{0,1:T(8,128)(2,1)S(1)}, bf16[384,1440]{0,1:T(8,128)(2,1)}, u32[]{:S(2)}) copy-start(bf16[384,1440]{0,1:T(8,128)(2,1)} %param.11) | copy-start | bytes 3317764
  7.2 155.1 %all-gather.7.cloned.1.call-start = ((), (), s32[]{:S(2)}) async-start(), calls=%async_computation.7 | async-start | bytes 5308416 | tf_op jit(solution)/shard_map/all_gather | solution.py:61
  27.5 3.6 copy-start
  92.2 104.8 %all-gather.5.cloned.1.call-start = ((), (), s32[]{:S(2)}) async-start(), calls=%async_computation.6 | async-start | bytes 5308416 | tf_op jit(solution)/shard_map/all_gather | solution.py:62
  144.2 3.9 copy-start.9
  148.1 174.5 %reduce-scatter.4.cloned.1.call-start = ((), (), s32[]{:S(2)}) async-start(), calls=%async_computation.8 | async-start | bytes 5529600
  206.8 11.2 %copy-start.4 = (bf16[2880,576]{0,1:T(8,128)(2,1)S(1)}, bf16[2880,576]{0,1:T(8,128)(2,1)}, u32[]{:S(2)}) copy-start(bf16[2880,576]{0,1:T(8,128)(2,1)} %reshape.349) | copy-start | bytes 9953284
  206.8 11.2 %copy-start.8 = (f32[576]{0:T(1024)S(1)}, f32[576]{0:T(1024)}, u32[]{:S(2)}) copy-start(f32[576]{0:T(1024)} %reshape.296) | copy-start | bytes 6916
  218.0 19.8 %copy-start.1 = (bf16[2880,576]{0,1:T(8,128)(2,1)S(1)}, bf16[2880,576]{0,1:T(8,128)(2,1)}, u32[]{:S(2)}) copy-start(bf16[2880,576]{0,1:T(8,128)(2,1)} %reshape.351) | copy-start | bytes 9953284
  250.3 9.3 %copy-start.10 = (bf16[576,1440]{1,0:T(8,128)(2,1)}, bf16[576,1440]{1,0:T(8,128)(2,1)S(1)}, u32[]{:S(2)}) copy-start(bf16[576,1440]{1,0:T(8,128)(2,1)S(1)} %get-tuple-element.31) | copy-start | bytes 4976644
  272.9 0.7 copy-start.7
  273.6 21.9 %copy-start.2 = (bf16[2880,576]{0,1:T(8,128)(2,1)S(1)}, bf16[2880,576]{0,1:T(8,128)(2,1)}, u32[]{:S(2)}) copy-start(bf16[2880,576]{0,1:T(8,128)(2,1)} %reshape.351) | copy-start | bytes 9953284
  288.2 38.5 %all-to-all-start.4 = ((bf16[16,1,36]{2,1,0:T(2,128)(2,1)}), bf16[16,1,36]{2,1,0:T(2,128)(2,1)S(1)}, u32[]{:S(2)}, u32[]{:S(2)}) async-start(bf16[16,1,36]{2,1,0:T(2,128)(2,1)} %all_to_all.29), calls=%async_computation.4 | async-start | bytes 16384 | tf_op jit(solution)/shard_map/all_to_all | solution.py:111
  326.8 7.1 %copy-start.3 = (bf16[2880,576]{0,1:T(8,128)(2,1)S(1)}, bf16[2880,576]{0,1:T(8,128)(2,1)}, u32[]{:S(2)}) copy-start(bf16[2880,576]{0,1:T(8,128)(2,1)} %reshape.351) | copy-start | bytes 9953284
  326.8 51.7 %all-to-all-start.3 = ((bf16[16,36,1440]{2,1,0:T(8,128)(2,1)}), bf16[16,36,1440]{2,1,0:T(8,128)(2,1)}, u32[]{:S(2)}, u32[]{:S(2)}) async-start(bf16[16,36,1440]{2,1,0:T(8,128)(2,1)} %reshape.293), calls=%async_computation.3 | async-start | bytes 3932160 | tf_op jit(solution)/shard_map/all_to_all | solution.py:104
  333.9 11.0 %copy-start.5 = (bf16[2880,576]{0,1:T(8,128)(2,1)S(1)}, bf16[2880,576]{0,1:T(8,128)(2,1)}, u32[]{:S(2)}) copy-start(bf16[2880,576]{0,1:T(8,128)(2,1)} %reshape.349) | copy-start | bytes 9953284
  333.9 11.0 %copy-start.11 = (bf16[576,1440]{1,0:T(8,128)(2,1)S(1)}, bf16[576,1440]{1,0:T(8,128)(2,1)}, u32[]{:S(2)}) copy-start(bf16[576,1440]{1,0:T(8,128)(2,1)} %get-tuple-element.29) | copy-start | bytes 4976644
Sparse Core Ops, SparseCore 0:
  92.3 48.7 all-gather.6
  148.2 48.7 all-gather.4
  273.1 49.4 reduce-scatter.3
where the time goes:
time: 421 us; the launch traced here: 414 us
  blocking collectives  114 us (27%)
  matrix products  103 us (24%)
  local copies, waits for them, and re-layouts  93.4 us (22%)
  waiting for transfers between devices  54.4 us (13%)
  other arithmetic  20.1 us (5%)
  starting transfers between devices  14.5 us (3%)
  between operations  14.5 us (3%)
    all_to_all x1, blocking collectives, shards(): lax.all_to_all(send_x, 'dp', split_axis=0, concat_axis=0, tiled=True)  50.9 us
    all_to_all x1, blocking collectives, shards(): lax.all_to_all(send_d, 'dp', split_axis=0, concat_axis=0, tiled=True)  49.4 us
    all_gather x1, waiting for transfers between devices, shards(): lax.all_gather(got_d.reshape(owners * capacity, part_width), 'tensor', ax...  25 us
    dot_general x1, matrix products, shards(): lax.dot_general(rows_d, down_w, contract_cols, preferred_element_type=jnp...  19.8 us
    unnamed x32, local copies, waits for them, and re-layouts  19.4 us
    unnamed x4, waiting for transfers between devices  16.3 us
    gather x2, local copies, waits for them, and re-layouts, shards(): jnp.take(back_rows, safe_target, axis=0)  15.2 us
    all_to_all x1, waiting for transfers between devices, shards(): lax.all_to_all(input_rows.reshape(owners, capacity, part_cols), 'dp', spl...  13.1 us
  transfers between devices with their start and end apart: 5, of which 3 were waited for; matrix products, arithmetic and copies ran while one was open for 19% of the time, Pallas kernels for 0%

commit v1 on v0

--- a/solution.py
+++ b/solution.py
@@ -59,7 +59,9 @@
     )
     rows_x, rows_d = (
         lax.all_gather(got_x.reshape(owners * capacity, part_width), "tensor", axis=1, tiled=True),
-        lax.all_gather(got_d.reshape(owners * capacity, part_width), "tensor", axis=1, tiled=True),
+        jnp.concatenate(
+            lax.all_gather(got_d.reshape(owners * capacity, part_width), "tensor"), axis=1
+        ),
     )
     prob_column = got_p.reshape(-1).astype(jnp.float32)[:, None]
     gate_w = w_gate[0]

time: 421 us -> 421 us (level)
    reshape x1 -> x2, local copies, waits for them, and re-layouts: 3.81 us -> 9.79 us  [shards(): jnp.concatenate(lax.all_gather(got_d.reshape(owners * capacity, part_widt...]
    all_gather x1 -> x0, local copies, waits for them, and re-layouts: 5.64 us -> none  [shards(): lax.all_gather(got_d.reshape(owners * capacity, part_width), 'tensor', ax...]
    unnamed x32 -> x31, local copies, waits for them, and re-layouts: 19.4 us -> 15.2 us
where the time goes in v1:
time: 421 us; the launch traced here: 414 us
  blocking collectives  114 us (27%)
  matrix products  103 us (24%)
  local copies, waits for them, and re-layouts  93.4 us (22%)
  waiting for transfers between devices  54.4 us (13%)
  other arithmetic  20.1 us (5%)
  starting transfers between devices  14.5 us (3%)
  between operations  14.5 us (3%)
    all_to_all x1, blocking collectives, shards(): lax.all_to_all(send_x, 'dp', split_axis=0, concat_axis=0, tiled=True)  50.9 us
    all_to_all x1, blocking collectives, shards(): lax.all_to_all(send_d, 'dp', split_axis=0, concat_axis=0, tiled=True)  49.4 us
    all_gather x1, waiting for transfers between devices, shards(): lax.all_gather(got_d.reshape(owners * capacity, part_width), 'tensor')  25 us
    dot_general x1, matrix products, shards(): lax.dot_general(rows_d, down_w, contract_cols, preferred_element_type=jnp...  19.8 us
    unnamed x4, waiting for transfers between devices  16.3 us
    unnamed x31, local copies, waits for them, and re-layouts  15.2 us
    gather x2, local copies, waits for them, and re-layouts, shards(): jnp.take(back_rows, safe_target, axis=0)  15.2 us
    all_to_all x1, waiting for transfers between devices, shards(): lax.all_to_all(input_rows.reshape(owners, capacity, part_cols), 'dp', spl...  13.1 us
  transfers between devices with their start and end apart: 5, of which 3 were waited for; matrix products, arithmetic and copies ran while one was open for 19% of the time, Pallas kernels for 0%

profile of v1, /device:TPU:13, one launch (start us, length us, event | category | flops | bytes accessed | tf_op | source)
XLA Modules:
  0.0 413.7 jit_solution(8770292031321615427)
XLA Ops:
  7.2 0.9 select_reduce_fusion.1
  8.2 0.1 copy.36
  8.3 0.2 reshape.290
  8.4 0.1 reshape.288
  8.6 0.1 reshape.287
  8.8 4.5 %reduce-window.6 = s32[16,12,128]{2,1,0:T(8,128)S(1)} reduce-window(s32[16,12,128]{2,1,0:T(8,128)S(1)} %fusion.30, s32[]{:T(128)} %constant.77.clone.1), window={size=1x1x128 pad=0_0x0_0x127_0}, to_apply=%region_1.2 | reduce-window | flops 3121152 | bytes 196612 | tf_op jit(solution)/shard_map/reduce-window
  13.4 0.4 slice_reduce_fusion
  13.8 0.2 reduce-window.9
  14.0 0.1 broadcast_add_fusion
  14.2 0.7 fusion.40
  14.8 6.2 %scatter_custom_fusion = s32[576]{0:T(1024)S(1)} fusion(s32[1536]{0:T(1024)S(1)} %get-tuple-element.22, s32[1536]{0:T(1024)S(1)} %iota.15, s32[]{:T(128)} %constant.82.clone.1), kind=kCustom, calls=%fused_computation.111 | custom fusion | bytes 2308 | tf_op jit(solution)/shard_map/scatter | solution.py:27
  21.1 1.6 copy.45
  22.7 1.2 copy.43
  23.9 3.6 gather_fusion.4
  27.5 3.6 gather_fusion.3
  31.1 3.8 select_select_fusion
  34.8 2.6 reshape.295
  37.5 50.9 %all_to_all.35 = bf16[16,36,1440]{2,1,0:T(8,128)(2,1)} all-to-all(bf16[16,36,1440]{2,1,0:T(8,128)(2,1)S(1)} %reshape.295), channel_id=1, replica_groups=mesh['dp'=16,'tensor'=2] {'dp'}, dimensions={0} | all-to-all | bytes 3317760 | tf_op jit(solution)/shard_map/all_to_all | solution.py:54
  88.4 3.8 reshape.296
  92.2 2.6 reshape.292
  94.9 49.4 %all_to_all.36 = bf16[16,36,1440]{2,1,0:T(8,128)(2,1)} all-to-all(bf16[16,36,1440]{2,1,0:T(8,128)(2,1)S(1)} %reshape.292), channel_id=1, replica_groups=mesh['dp'=16,'tensor'=2] {'dp'}, dimensions={0} | all-to-all | bytes 3317760 | tf_op jit(solution)/shard_map/all_to_all | solution.py:55
  144.2 3.8 all_gather_reshape.3
  148.1 0.2 copy.41
  148.3 0.2 reshape.291
  148.5 3.9 gather_fusion
  152.5 0.1 all_to_all.28
  152.6 9.0 %all_to_all.37 = bf16[16,1,36]{2,1,0:T(2,128)(2,1)S(1)} all-to-all(bf16[16,1,36]{2,1,0:T(2,128)(2,1)S(1)} %all_to_all.28), channel_id=1, replica_groups=mesh['dp'=16,'tensor'=2] {'dp'}, dimensions={0} | all-to-all | bytes 2304 | tf_op jit(solution)/shard_map/all_to_all | solution.py:56
  161.6 0.7 reshape.300
  162.2 5.6 %copy.46 = bf16[2,1440,576]{1,0,2:T(2,128)(2,1)S(1)} copy(bf16[2,1440,576]{1,2,0:T(8,128)(2,1)} %all-gather.6.cloned.1.call-done) | data formatting | bytes 6635520 | tf_op jit(solution)/shard_map/all_gather | solution.py:61
  167.9 4.1 %reshape.353 = bf16[2880,576]{0,1:T(8,128)(2,1)} reshape(bf16[2,1440,576]{1,0,2:T(2,128)(2,1)S(1)} %copy.46) | data formatting | bytes 6635520
  172.0 25.0 %all-gather.4.cloned.1.call-done = bf16[2,576,1440]{2,1,0:T(8,128)(2,1)} async-done(((bf16[1,576,1440]{2,1,0:T(8,128)(2,1)}), bf16[2,576,1440]{2,1,0:T(8,128)(2,1)}) %all-gather.4.cloned.1.call-update) | async-done | bytes 3317776 | tf_op jit(solution)/shard_map/all_gather | solution.py:63
  197.0 5.6 %copy.44 = bf16[576,2,1440]{2,1,0:T(2,128)(2,1)S(1)} copy(bf16[576,2,1440]{2,0,1:T(8,128)(2,1)} %bitcast.71) | data formatting | bytes 6635520 | tf_op jit(solution)/shard_map/reshape | solution.py:62
  202.7 4.2 %reshape.294 = bf16[576,2880]{1,0:T(8,128)(2,1)} reshape(bf16[576,2,1440]{2,1,0:T(2,128)(2,1)S(1)} %copy.44) | data formatting | bytes 6635520 | tf_op jit(solution)/shard_map/reshape | solution.py:62
  206.8 11.2 %fusion.5 = f32[576,1440]{1,0:T(8,128)} fusion(bf16[2880,576]{0,1:T(8,128)(2,1)} %reshape.353, bf16[1,2880,1440]{1,2,0:T(8,128)(2,1)} %param.15), kind=kOutput, calls=%fused_computation.14 | convolution fusion | flops 4777574400 | bytes 14929920 | tf_op jit(solution)/shard_map/dot_general | solution.py:72
  218.0 19.8 %fusion.21 = f32[576,1440]{1,0:T(8,128)S(1)} fusion(bf16[576,2880]{1,0:T(8,128)(2,1)S(1)} %copy-done.4, bf16[1,1440,2880]{2,1,0:T(8,128)(2,1)} %param.17, f32[576]{0:T(1024)S(1)} %copy-done.8), kind=kOutput, calls=%fused_computation.30 | convolution fusion | flops 4778403840 | bytes 14932224 | tf_op jit(solution)/shard_map/dot_general | solution.py:76
  237.8 12.5 %multiply_convert_fusion = (bf16[576,1440]{1,0:T(8,128)(2,1)}, bf16[576,1440]{1,0:T(8,128)(2,1)}, bf16[576,1440]{1,0:T(8,128)(2,1)S(1)}) fusion(f32[576,1440]{1,0:T(8,128)} %fusion.5, f32[576,1440]{1,0:T(8,128)S(1)} %fusion.21, bf16[2880,576]{0,1:T(8,128)(2,1)S(1)} %copy-done.1, bf16[1,2880,1440]{1,2,0:T(8,128)(2,1)} %param.16), kind=kOutput, calls=%fused_computation.31 | convolution fusion | flops 4792504320 | bytes 23224320 | tf_op jit(solution)/shard_map/dot_general | solution.py:73
  250.3 9.3 %fusion.3 = f32[576,2880]{1,0:T(8,128)S(1)} fusion(bf16[576,1440]{1,0:T(8,128)(2,1)} %get-tuple-element.30, bf16[1,2880,1440]{1,2,0:T(8,128)(2,1)} %param.15), kind=kOutput, calls=%fused_computation.12 | convolution fusion | flops 4777574400 | bytes 16588800 | tf_op jit(solution)/shard_map/dot_general | solution.py:97
  259.7 9.5 %add_convert_fusion = bf16[576,2880]{1,0:T(8,128)(2,1)S(1)} fusion(f32[576,2880]{1,0:T(8,128)S(1)} %fusion.3, bf16[576,1440]{1,0:T(8,128)(2,1)S(1)} %get-tuple-element.31, bf16[1,2880,1440]{1,2,0:T(8,128)(2,1)} %param.16), kind=kOutput, calls=%fused_computation.28 | convolution fusion | flops 4780892160 | bytes 19906560 | tf_op jit(solution)/shard_map/dot_general | solution.py:99
  269.2 3.7 copy.50
  273.0 0.2 reduce_sum.45
  273.2 0.4 copy-done.7
  273.6 9.5 %fusion.16 = f32[576]{0:T(1024)S(1)} fusion(bf16[576,2880]{1,0:T(8,128)(2,1)} %reshape.294, bf16[576,1440]{1,0:T(8,128)(2,1)} %get-tuple-element.29, bf16[1,1440,2880]{2,1,0:T(8,128)(2,1)} %param.17), kind=kOutput, calls=%fused_computation.27 | convolution fusion | flops 4782550528 | bytes 13273344 | tf_op jit(solution)/shard_map/dot_general | solution.py:77
  283.1 4.4 %psum.7 = bf16[576]{0:T(1024)(128)(2,1)S(1)} all-reduce(f32[576]{0:T(1024)S(1)} %fusion.16), channel_id=1, replica_groups=mesh['dp'=16,'tensor'=2] {'tensor'}, use_global_device_ids=true, to_apply=%region_8.10 | all-reduce | flops 576 | bytes 3456 | tf_op jit(solution)/shard_map/psum | solution.py:79
  287.5 0.7 all_to_all.29
  288.2 7.3 %all-to-all-start.4 = ((bf16[16,1,36]{2,1,0:T(2,128)(2,1)}), bf16[16,1,36]{2,1,0:T(2,128)(2,1)S(1)}, u32[]{:S(2)}, u32[]{:S(2)}) async-start(bf16[16,1,36]{2,1,0:T(2,128)(2,1)} %all_to_all.29), calls=%async_computation.4 | async-start | bytes 16384 | tf_op jit(solution)/shard_map/all_to_all | solution.py:113
  295.5 10.8 %fusion.2 = bf16[1,2880,1440]{1,2,0:T(8,128)(2,1)} fusion(bf16[2880,576]{0,1:T(8,128)(2,1)S(1)} %copy-done.2, bf16[576,1440]{1,0:T(8,128)(2,1)} %copy-done.10), kind=kOutput, calls=%fused_computation.11 | convolution fusion | flops 4781721600 | bytes 13271040 | tf_op jit(solution)/shard_map/dot_general | solution.py:94
  306.3 16.3 %reduce-scatter.4.cloned.1.call-done = bf16[1440,576]{1,0:T(8,128)(2,1)} async-done(((bf16[2880,576]{1,0:T(8,128)(2,1)}), bf16[1440,576]{1,0:T(8,128)(2,1)}) %reduce-scatter.4.cloned.1.call-update) | async-done | bytes 1658896
  322.6 2.6 copy.51
  325.2 1.6 reshape.297
  326.8 7.1 %all-to-all-start.3 = ((bf16[16,36,1440]{2,1,0:T(8,128)(2,1)}), bf16[16,36,1440]{2,1,0:T(8,128)(2,1)}, u32[]{:S(2)}, u32[]{:S(2)}) async-start(bf16[16,36,1440]{2,1,0:T(8,128)(2,1)} %reshape.297), calls=%async_computation.3 | async-start | bytes 3932160 | tf_op jit(solution)/shard_map/all_to_all | solution.py:106
  333.9 10.9 %fusion.1 = bf16[1,2880,1440]{1,2,0:T(8,128)(2,1)} fusion(bf16[2880,576]{0,1:T(8,128)(2,1)S(1)} %copy-done.3, bf16[576,1440]{1,0:T(8,128)(2,1)} %get-tuple-element.30), kind=kOutput, calls=%fused_computation.10 | convolution fusion | flops 4781721600 | bytes 13271040 | tf_op jit(solution)/shard_map/dot_general | solution.py:91
  344.9 9.5 %fusion = bf16[1,1440,2880]{2,1,0:T(8,128)(2,1)} fusion(bf16[576,1440]{1,0:T(8,128)(2,1)S(1)} %copy-done.11, bf16[576,2880]{1,0:T(8,128)(2,1)S(1)} %copy-done.5, f32[576]{0:T(1024)S(1)} %copy-done.8), kind=kOutput, calls=%fused_computation.9 | convolution fusion | flops 4786698240 | bytes 13273344 | tf_op jit(solution)/shard_map/dot_general | solution.py:88
  354.4 0.1 reshape.299
  354.5 9.5 %gather_fusion.2 = bf16[1536]{0:T(1024)(128)(2,1)S(1)} fusion(bf16[576]{0:T(1024)(128)(2,1)S(1)} %reshape.299, s32[2048]{0:T(1024)S(1)} %pad_clamp_fusion), kind=kCustom, calls=%fused_computation.4 | custom fusion | bytes 12288 | tf_op jit(solution)/shard_map/gather | solution.py:128
  364.0 0.2 gather.21
  364.3 0.6 broadcast_select_fusion
  364.9 0.2 copy.35
  365.1 0.2 copy.39
  365.3 13.1 %all-to-all-done.3 = bf16[16,36,1440]{2,1,0:T(8,128)(2,1)} async-done(((bf16[16,36,1440]{2,1,0:T(8,128)(2,1)}), bf16[16,36,1440]{2,1,0:T(8,128)(2,1)}, u32[]{:S(2)}, u32[]{:S(2)}) %all-to-all-start.3) | async-done | bytes 1658912 | tf_op jit(solution)/shard_map/all_to_all | solution.py:106
  378.5 2.7 reshape.298
  381.2 6.2 %gather_fusion.1 = bf16[1536,1440]{1,0:T(8,128)(2,1)} fusion(bf16[576,1440]{1,0:T(8,128)(2,1)S(1)} %reshape.298, s32[2048]{0:T(1024)S(1)} %pad_clamp_fusion), kind=kCustom, calls=%fused_computation.3 | custom fusion | bytes 8853504 | tf_op jit(solution)/shard_map/jit(_take)/gather | solution.py:124
  387.4 8.9 %gather.19 = bf16[384,4,1440]{2,1,0:T(4,128)(2,1)} reshape(bf16[1536,1440]{1,0:T(8,128)(2,1)} %gather_fusion.1) | data formatting | bytes 8847360 | tf_op jit(solution)/shard_map/jit(_take)/gather | solution.py:124
  396.3 9.1 %select_reduce_fusion = bf16[384,1440]{1,0:T(8,128)(2,1)S(1)} fusion(bf16[384,4,1440]{2,1,0:T(4,128)(2,1)} %gather.19, pred[384,4]{1,0:T(8,128)(4,1)S(1)} %copy.39, pred[384,4]{1,0:T(8,128)(4,1)S(1)} %copy.35), kind=kLoop, calls=%fused_computation.29 | loop fusion | flops 6082560 | bytes 5532672 | tf_op jit(solution)/shard_map/reduce_sum | solution.py:125
  405.4 1.4 copy.49
  (49 shorter events, 0.6 us)
Async XLA Ops:
  7.2 15.5 %copy-start.6 = (bf16[384,1440]{0,1:T(8,128)(2,1)S(1)}, bf16[384,1440]{0,1:T(8,128)(2,1)}, u32[]{:S(2)}) copy-start(bf16[384,1440]{0,1:T(8,128)(2,1)} %param.11) | copy-start | bytes 3317764
  7.2 155.1 %all-gather.6.cloned.1.call-start = ((), (), s32[]{:S(2)}) async-start(), calls=%async_computation.7 | async-start | bytes 5308416 | tf_op jit(solution)/shard_map/all_gather | solution.py:61
  27.5 3.6 copy-start
  92.2 104.8 %all-gather.4.cloned.1.call-start = ((), (), s32[]{:S(2)}) async-start(), calls=%async_computation.6 | async-start | bytes 5308416 | tf_op jit(solution)/shard_map/all_gather | solution.py:63
  144.2 3.9 copy-start.9
  148.1 174.5 %reduce-scatter.4.cloned.1.call-start = ((), (), s32[]{:S(2)}) async-start(), calls=%async_computation.8 | async-start | bytes 5529600
  206.8 11.2 %copy-start.4 = (bf16[576,2880]{1,0:T(8,128)(2,1)S(1)}, bf16[576,2880]{1,0:T(8,128)(2,1)}, u32[]{:S(2)}) copy-start(bf16[576,2880]{1,0:T(8,128)(2,1)} %reshape.294) | copy-start | bytes 9953284
  206.8 11.2 %copy-start.8 = (f32[576]{0:T(1024)S(1)}, f32[576]{0:T(1024)}, u32[]{:S(2)}) copy-start(f32[576]{0:T(1024)} %reshape.300) | copy-start | bytes 6916
  218.0 19.8 %copy-start.1 = (bf16[2880,576]{0,1:T(8,128)(2,1)S(1)}, bf16[2880,576]{0,1:T(8,128)(2,1)}, u32[]{:S(2)}) copy-start(bf16[2880,576]{0,1:T(8,128)(2,1)} %reshape.353) | copy-start | bytes 9953284
  250.3 9.3 %copy-start.10 = (bf16[576,1440]{1,0:T(8,128)(2,1)}, bf16[576,1440]{1,0:T(8,128)(2,1)S(1)}, u32[]{:S(2)}) copy-start(bf16[576,1440]{1,0:T(8,128)(2,1)S(1)} %get-tuple-element.31) | copy-start | bytes 4976644
  272.9 0.7 copy-start.7
  273.6 21.9 %copy-start.2 = (bf16[2880,576]{0,1:T(8,128)(2,1)S(1)}, bf16[2880,576]{0,1:T(8,128)(2,1)}, u32[]{:S(2)}) copy-start(bf16[2880,576]{0,1:T(8,128)(2,1)} %reshape.353) | copy-start | bytes 9953284
  288.2 38.5 %all-to-all-start.4 = ((bf16[16,1,36]{2,1,0:T(2,128)(2,1)}), bf16[16,1,36]{2,1,0:T(2,128)(2,1)S(1)}, u32[]{:S(2)}, u32[]{:S(2)}) async-start(bf16[16,1,36]{2,1,0:T(2,128)(2,1)} %all_to_all.29), calls=%async_computation.4 | async-start | bytes 16384 | tf_op jit(solution)/shard_map/all_to_all | solution.py:113
  326.8 7.1 %copy-start.3 = (bf16[2880,576]{0,1:T(8,128)(2,1)S(1)}, bf16[2880,576]{0,1:T(8,128)(2,1)}, u32[]{:S(2)}) copy-start(bf16[2880,576]{0,1:T(8,128)(2,1)} %reshape.353) | copy-start | bytes 9953284
  326.8 51.7 %all-to-all-start.3 = ((bf16[16,36,1440]{2,1,0:T(8,128)(2,1)}), bf16[16,36,1440]{2,1,0:T(8,128)(2,1)}, u32[]{:S(2)}, u32[]{:S(2)}) async-start(bf16[16,36,1440]{2,1,0:T(8,128)(2,1)} %reshape.297), calls=%async_computation.3 | async-start | bytes 3932160 | tf_op jit(solution)/shard_map/all_to_all | solution.py:106
  333.9 11.0 %copy-start.5 = (bf16[576,2880]{1,0:T(8,128)(2,1)S(1)}, bf16[576,2880]{1,0:T(8,128)(2,1)}, u32[]{:S(2)}) copy-start(bf16[576,2880]{1,0:T(8,128)(2,1)} %reshape.294) | copy-start | bytes 9953284
  333.9 11.0 %copy-start.11 = (bf16[576,1440]{1,0:T(8,128)(2,1)S(1)}, bf16[576,1440]{1,0:T(8,128)(2,1)}, u32[]{:S(2)}) copy-start(bf16[576,1440]{1,0:T(8,128)(2,1)} %get-tuple-element.29) | copy-start | bytes 4976644
Sparse Core Ops, SparseCore 0:
  92.3 48.7 all-gather.5
  148.2 48.7 all-gather.3
  273.1 49.4 reduce-scatter.3
